TPU v7x, 512 devices: a whole 4x8x8 slice. The times are simulated.
512 devices in a mesh: seq: 32 (over x, y), head: 16 (over z, core).
Axes of the slice: x: 4, y: 8, z: 8, core: 2. Of those that a mesh axis runs over, the one named last changes fastest.
Arguments:
- slab_query: bfloat16 [4096, 8192], P('seq', 'head'), may hold values from -6 to 6
- slab_key: bfloat16 [4096, 8192], P('seq', 'head'), may hold values from -6 to 6
- slab_value: bfloat16 [4096, 8192], P('seq', 'head'), may hold values from -6 to 6
- slab_levels: bfloat16 [6, 64, 4096], P(None, 'head', 'seq'), may hold values from 0.1 to 10
- norm_gain: bfloat16 [8192], P('head'), may hold values from 0.5 to 1.5
- user_query: bfloat16 [512, 64, 8192], P('seq', None, 'head'), may hold values from -6 to 6
- user_key: bfloat16 [512, 64, 8192], P('seq', None, 'head'), may hold values from -6 to 6
- user_value: bfloat16 [512, 64, 8192], P('seq', None, 'head'), may hold values from -6 to 6
- user_levels: bfloat16 [512, 6, 64, 64], P('seq', None, 'head'), may hold values from 0.1 to 10
- prefix_lengths: int32 [512], P('seq'), may hold values from 1 to 31, as said below
Outputs:
- slab_out: bfloat16 [4096, 8192], P('seq', 'head')
- user_out: bfloat16 [512, 64, 8192], P('seq', None, 'head')
Inputs may be any that keep to these rules, and one draw needn't show every extreme that they name: `prefix_lengths`: the 16 users that lie on one index of seq have distinct prefix lengths; one prefix length is held by one user of every index of seq.
All inputs are finite; a program needn't handle non-finite values.
Results may differ from a plain program's by a relative error of at most 0.012.
Values may be sent and summed in bfloat16 or wider, within the bound.
A program may use at most 64 MiB of HBM per device.

v0:
```python
import jax
import jax.numpy as jnp
from jax import lax
from jax.sharding import PartitionSpec as P

HEADS = 64
HD = 128


def partner_2(value, axis, bit):
    mask = 2**bit
    pairs = [(source, source ^ mask) for source in range(lax.axis_size(axis))]
    return lax.ppermute(value, axis, pairs)


def local_part(query_rows, key_rows, value_rows, first_weights):
    scores = jnp.einsum("bthd,bshd->bhts", query_rows, key_rows, preferred_element_type=jnp.float32)
    token_count = query_rows.shape[1]
    causal_mask = jnp.arange(token_count)[:, None] >= jnp.arange(token_count)[None, :]
    scores = jnp.where(causal_mask, scores, jnp.zeros_like(scores)).astype(jnp.bfloat16)
    result = jnp.einsum("bhts,bshd->bthd", scores, value_rows, preferred_element_type=jnp.float32)
    return result * jnp.transpose(first_weights, (0, 2, 1)).astype(jnp.float32)[..., None]


def read_prefix(query_rows, level_weights, node_states):
    level_count, head_count, inner, outer = node_states.shape
    merged = jnp.transpose(node_states, (1, 2, 0, 3)).reshape(
        head_count, inner, level_count * outer
    )
    projected = jnp.einsum("bthd,hdf->bthf", query_rows, merged, preferred_element_type=jnp.float32)
    projected = projected.reshape(projected.shape[:3] + (level_count, outer))
    scale_rows = jnp.transpose(level_weights, (0, 3, 2, 1)).astype(jnp.float32)[..., None]
    return jnp.sum(projected * scale_rows, axis=3)


def read_blocks(held_query, held_weights, node_states, head_count):
    slot_count, suffix, width = held_query.shape
    group_size = min(8, slot_count)
    grouped_query = held_query.reshape(slot_count // group_size, group_size, suffix, head_count, HD)
    grouped_weights = held_weights.reshape(
        (slot_count // group_size, group_size) + held_weights.shape[1:]
    )

    def one_group(packed):
        return read_prefix(packed[0], packed[1], node_states).astype(jnp.bfloat16)

    answers = lax.map(one_group, (grouped_query, grouped_weights))
    return answers.reshape(slot_count, suffix, width)


def local(
    slab_query,
    slab_key,
    slab_value,
    slab_levels,
    norm_gain,
    user_query,
    user_key,
    user_value,
    user_levels,
    prefix_lengths,
):
    seq_count = lax.axis_size("seq")
    tree_depth = seq_count.bit_length() - 1
    position = lax.axis_index("seq")
    token_count, width = slab_query.shape
    head_count = width // HD
    user_count, suffix = (user_query.shape[0], user_query.shape[1])
    slab_queries = slab_query.reshape(1, token_count, head_count, HD)
    slab_keys = slab_key.reshape(1, token_count, head_count, HD)
    slab_values = slab_value.reshape(1, token_count, head_count, HD)
    user_queries = user_query.reshape(user_count, suffix, head_count, HD)
    user_keys = user_key.reshape(user_count, suffix, head_count, HD)
    user_values = user_value.reshape(user_count, suffix, head_count, HD)
    block_state = jnp.einsum(
        "thd,the->hde", slab_keys[0], slab_values[0], preferred_element_type=jnp.float32
    ).astype(jnp.bfloat16)
    slab_local = local_part(slab_queries, slab_keys, slab_values, slab_levels[0][None])
    user_local = local_part(user_queries, user_keys, user_values, user_levels[:, 0])
    slab_weights = slab_levels[1 : 1 + tree_depth][None]
    user_weights = user_levels[:, 1 : 1 + tree_depth]
    running = block_state.astype(jnp.float32)
    collected = []
    for bit_index in range(tree_depth):
        partner = partner_2(running, "seq", bit_index)
        upper = jnp.bitwise_and(jnp.right_shift(position, bit_index), 1)
        collected.append(jnp.where(upper == 1, partner, jnp.zeros_like(partner)))
        running = running + partner
    node_states = jnp.stack(collected).astype(jnp.bfloat16)
    send_query = (
        jnp.zeros((seq_count, suffix, width), jnp.bfloat16).at[prefix_lengths].set(user_query)
    )
    send_weights = (
        jnp.zeros((seq_count,) + user_weights.shape[1:], jnp.bfloat16)
        .at[prefix_lengths]
        .set(user_weights)
    )
    held_query, held_weights = (
        lax.all_to_all(send_query, "seq", split_axis=0, concat_axis=0, tiled=True),
        lax.all_to_all(send_weights, "seq", split_axis=0, concat_axis=0, tiled=True),
    )
    answers = read_blocks(held_query, held_weights, node_states, head_count)
    returned = lax.all_to_all(answers, "seq", split_axis=0, concat_axis=0, tiled=True)
    user_prefix = returned[prefix_lengths].reshape(user_count, suffix, head_count, HD)
    slab_total = slab_local + read_prefix(slab_queries, slab_weights, node_states)
    user_total = user_local + user_prefix.astype(jnp.float32)
    slab_square = jnp.sum(slab_total * slab_total, axis=(2, 3))
    user_square = jnp.sum(user_total * user_total, axis=(2, 3))
    slab_square, user_square = lax.psum((slab_square, user_square), "head")
    gain_rows = norm_gain.reshape(head_count, HD).astype(jnp.float32)
    slab_root = jnp.sqrt(slab_square / (HEADS * HD) + 1e-06)
    user_root = jnp.sqrt(user_square / (HEADS * HD) + 1e-06)
    slab_out = (
        (slab_total / slab_root[..., None, None] * gain_rows)
        .astype(jnp.bfloat16)
        .reshape(token_count, width)
    )
    user_out = (
        (user_total / user_root[..., None, None] * gain_rows)
        .astype(jnp.bfloat16)
        .reshape(user_count, suffix, width)
    )
    return (slab_out, user_out)


def solution(mesh):
    return jax.shard_map(
        local,
        mesh=mesh,
        in_specs=(
            P("seq", "head"),
            P("seq", "head"),
            P("seq", "head"),
            P(None, "head", "seq"),
            P("head"),
            P("seq", None, "head"),
            P("seq", None, "head"),
            P("seq", None, "head"),
            P("seq", None, "head", None),
            P("seq"),
        ),
        out_specs=(P("seq", "head"), P("seq", None, "head")),
        check_vma=False,
    )
```

profile of v0, /device:TPU:1, one launch (start us, length us, event | category | flops | bytes accessed | tf_op | source)
XLA Modules:
  0.0 315.1 jit_solution(16962786662297436924)
XLA Ops:
  0.7 0.8 compare_select_fusion
  1.5 0.9 slice.15
  2.4 1.1 scatter_fusion.1
  3.6 0.8 reshape.168
  4.3 10.5 %all-to-all-start.1 = ((bf16[32,2,640]{2,1,0:T(2,128)(2,1)}), bf16[32,2,640]{2,1,0:T(2,128)(2,1)S(1)}, u32[]{:S(2)}, u32[]{:S(2)}) async-start(bf16[32,2,640]{2,1,0:T(2,128)(2,1)} %reshape.168), calls=%async_computation.1 | async-start | bytes 163840 | tf_op jit(solution)/shard_map/all_to_all | solution.py:100
  14.8 1.6 broadcast_in_dim.48
  16.4 3.0 scatter_fusion
  19.4 4.3 %all-to-all-done.1 = bf16[32,2,640]{2,1,0:T(2,128)(2,1)S(1)} async-done(((bf16[32,2,640]{2,1,0:T(2,128)(2,1)}), bf16[32,2,640]{2,1,0:T(2,128)(2,1)S(1)}, u32[]{:S(2)}, u32[]{:S(2)}) %all-to-all-start.1) | async-done | bytes 81952 | tf_op jit(solution)/shard_map/all_to_all | solution.py:100
  23.8 5.1 %all-to-all-start = ((bf16[32,64,512]{2,1,0:T(8,128)(2,1)}), bf16[32,64,512]{2,1,0:T(8,128)(2,1)}, u32[]{:S(2)}, u32[]{:S(2)}) async-start(bf16[32,64,512]{2,1,0:T(8,128)(2,1)} %scatter_fusion), calls=%async_computation | async-start | bytes 4194304 | tf_op jit(solution)/shard_map/all_to_all | solution.py:99
  29.2 3.1 collective-permute-start
  32.3 48.7 %collective-permute-done = f32[4,128,128]{2,1,0:T(8,128)S(1)} collective-permute-done((f32[4,128,128]{2,1,0:T(8,128)S(1)}, f32[4,128,128]{2,1,0:T(8,128)S(1)}, u32[]{:S(2)}, u32[]{:S(2)}) %collective-permute-start) | collective-permute-done | bytes 262176 | tf_op jit(solution)/shard_map/ppermute | solution.py:13
  81.0 3.1 collective-permute-start.1
  84.1 13.1 %collective-permute-done.1 = f32[4,128,128]{2,1,0:T(8,128)S(1)} collective-permute-done((f32[4,128,128]{2,1,0:T(8,128)S(1)}, f32[4,128,128]{2,1,0:T(8,128)S(1)}, u32[]{:S(2)}, u32[]{:S(2)}) %collective-permute-start.1) | collective-permute-done | bytes 262176 | tf_op jit(solution)/shard_map/ppermute | solution.py:13
  97.2 6.1 %collective-permute-start.2 = (f32[4,128,128]{2,1,0:T(8,128)S(1)}, f32[4,128,128]{2,1,0:T(8,128)S(1)}, u32[]{:S(2)}, u32[]{:S(2)}) collective-permute-start(f32[4,128,128]{2,1,0:T(8,128)S(1)} %add.43), channel_id=1, source_target_pairs={{0,64},{16,80},{32,96},{48,112},{64,0},{80,16},{96,32},{112,48},{1... | collective-permute-start | bytes 786440 | tf_op jit(solution)/shard_map/ppermute | solution.py:13
  103.6 12.1 %collective-permute-done.2 = f32[4,128,128]{2,1,0:T(8,128)S(1)} collective-permute-done((f32[4,128,128]{2,1,0:T(8,128)S(1)}, f32[4,128,128]{2,1,0:T(8,128)S(1)}, u32[]{:S(2)}, u32[]{:S(2)}) %collective-permute-start.2) | collective-permute-done | bytes 262176 | tf_op jit(solution)/shard_map/ppermute | solution.py:13
  115.8 3.2 %collective-permute-start.3 = (f32[4,128,128]{2,1,0:T(8,128)S(1)}, f32[4,128,128]{2,1,0:T(8,128)S(1)}, u32[]{:S(2)}, u32[]{:S(2)}) collective-permute-start(f32[4,128,128]{2,1,0:T(8,128)S(1)} %add.44), channel_id=1, source_target_pairs={{0,128},{16,144},{32,160},{48,176},{64,192},{80,208},{96,224},{112... | collective-permute-start | bytes 786440 | tf_op jit(solution)/shard_map/ppermute | solution.py:13
  119.0 4.8 %collective-permute-done.3 = f32[4,128,128]{2,1,0:T(8,128)S(1)} collective-permute-done((f32[4,128,128]{2,1,0:T(8,128)S(1)}, f32[4,128,128]{2,1,0:T(8,128)S(1)}, u32[]{:S(2)}, u32[]{:S(2)}) %collective-permute-start.3) | collective-permute-done | bytes 262176 | tf_op jit(solution)/shard_map/ppermute | solution.py:13
  123.9 4.5 %collective-permute-start.4 = (bf16[4,128,128]{2,1,0:T(8,128)(2,1)S(1)}, bf16[4,128,128]{2,1,0:T(8,128)(2,1)S(1)}, u32[]{:S(2)}, u32[]{:S(2)}) collective-permute-start(bf16[4,128,128]{2,1,0:T(8,128)(2,1)S(1)} %add.45), channel_id=1, source_target_pairs={{0,256},{16,272},{32,288},{48,304},{64,320},{80,336},{96,352},{112... | collective-permute-start | bytes 393224 | tf_op jit(solution)/shard_map/ppermute | solution.py:13
  128.5 2.6 collective-permute-done.4
  131.5 4.0 %reshape.129 = bf16[4,8,64,4,128]{4,3,2,1,0:T(4,128)(2,1)} reshape(bf16[32,64,512]{2,1,0:T(8,128)(2,1)} %all-to-all-done) | data formatting | bytes 4194304 | tf_op jit(solution)/shard_map/reshape | solution.py:39
  135.5 78.2 %while.10 = (s32[]{:T(128)}, bf16[4,8,64,4,128]{4,3,2,1,0:T(4,128)(2,1)}, bf16[4,8,64,4,128]{4,3,2,1,0:T(4,128)(2,1)}, bf16[5,4,128,128]{2,3,0,1:T(8,128)(2,1)S(...) while((s32[]{:T(128)}, bf16[4,8,64,4,128]{4,3,2,1,0:T(4,128)(2,1)}, ...), condition=%wide.region_7.8_spmd, body=%wide.region_5.7_spmd.sunk | while | flops 337913856 | bytes 35442776 | solution.py:47
  135.5 1.2 constant_dynamic-slice_fusion.4
  136.7 0.9 convolution_bitcast_fusion.3
  137.6 2.7 copy.146
  140.3 7.4 %reshape.171 = f32[8,64,4,5,128]{4,3,1,2,0:T(8,128)} reshape(f32[8,64,4,640]{3,1,2,0:T(8,128)} %copy.146) | data formatting | bytes 10485760 | tf_op jit(solution)/shard_map/while/body/eval_jaxpr/reshape | solution.py:31
  147.7 0.3 copy.147
  148.2 5.7 %multiply_reduce_fusion.5 = bf16[8,64,4,128]{3,1,2,0:T(8,128)(2,1)S(1)} fusion(f32[8,64,4,5,128]{4,3,1,2,0:T(8,128)} %reshape.171, f32[8,64,4,5]{3,1,2,0:T(8,128)S(1)} %convert_bitcast_fusion.8), kind=kLoop, calls=%fused_computation.3.clone.1 | loop fusion | flops 2359296 | bytes 5808128 | tf_op jit(solution)/shard_map/while/body/eval_jaxpr/reduce_sum | solution.py:33
  153.9 1.2 copy_dynamic-update-slice_fusion.2
  155.1 1.2 constant_dynamic-slice_fusion.4
  156.3 0.9 convolution_bitcast_fusion.3
  157.2 2.7 copy.146
  159.9 7.4 %reshape.171 = f32[8,64,4,5,128]{4,3,1,2,0:T(8,128)} reshape(f32[8,64,4,640]{3,1,2,0:T(8,128)} %copy.146) | data formatting | bytes 10485760 | tf_op jit(solution)/shard_map/while/body/eval_jaxpr/reshape | solution.py:31
  167.3 0.3 copy.147
  167.7 5.7 %multiply_reduce_fusion.5 = bf16[8,64,4,128]{3,1,2,0:T(8,128)(2,1)S(1)} fusion(f32[8,64,4,5,128]{4,3,1,2,0:T(8,128)} %reshape.171, f32[8,64,4,5]{3,1,2,0:T(8,128)S(1)} %convert_bitcast_fusion.8), kind=kLoop, calls=%fused_computation.3.clone.1 | loop fusion | flops 2359296 | bytes 5808128 | tf_op jit(solution)/shard_map/while/body/eval_jaxpr/reduce_sum | solution.py:33
  173.4 1.2 copy_dynamic-update-slice_fusion.2
  174.6 1.2 constant_dynamic-slice_fusion.4
  175.9 0.9 convolution_bitcast_fusion.3
  176.7 2.7 copy.146
  179.5 7.4 %reshape.171 = f32[8,64,4,5,128]{4,3,1,2,0:T(8,128)} reshape(f32[8,64,4,640]{3,1,2,0:T(8,128)} %copy.146) | data formatting | bytes 10485760 | tf_op jit(solution)/shard_map/while/body/eval_jaxpr/reshape | solution.py:31
  187.3 5.7 %multiply_reduce_fusion.5 = bf16[8,64,4,128]{3,1,2,0:T(8,128)(2,1)S(1)} fusion(f32[8,64,4,5,128]{4,3,1,2,0:T(8,128)} %reshape.171, f32[8,64,4,5]{3,1,2,0:T(8,128)S(1)} %convert_bitcast_fusion.8), kind=kLoop, calls=%fused_computation.3.clone.1 | loop fusion | flops 2359296 | bytes 5808128 | tf_op jit(solution)/shard_map/while/body/eval_jaxpr/reduce_sum | solution.py:33
  193.0 1.2 copy_dynamic-update-slice_fusion.2
  194.2 1.2 constant_dynamic-slice_fusion.4
  195.4 0.9 convolution_bitcast_fusion.3
  196.3 2.7 copy.146
  199.0 7.4 %reshape.171 = f32[8,64,4,5,128]{4,3,1,2,0:T(8,128)} reshape(f32[8,64,4,640]{3,1,2,0:T(8,128)} %copy.146) | data formatting | bytes 10485760 | tf_op jit(solution)/shard_map/while/body/eval_jaxpr/reshape | solution.py:31
  206.9 5.7 %multiply_reduce_fusion.5 = bf16[8,64,4,128]{3,1,2,0:T(8,128)(2,1)S(1)} fusion(f32[8,64,4,5,128]{4,3,1,2,0:T(8,128)} %reshape.171, f32[8,64,4,5]{3,1,2,0:T(8,128)S(1)} %convert_bitcast_fusion.8), kind=kLoop, calls=%fused_computation.3.clone.1 | loop fusion | flops 2359296 | bytes 5808128 | tf_op jit(solution)/shard_map/while/body/eval_jaxpr/reduce_sum | solution.py:33
  212.5 1.2 copy_dynamic-update-slice_fusion.2
  213.7 4.1 %reshape.131 = bf16[32,64,512]{2,1,0:T(8,128)(2,1)} reshape(bf16[4,8,64,4,128]{4,3,2,1,0:T(4,128)(2,1)} %get-tuple-element.29) | data formatting | bytes 4194304 | tf_op jit(solution)/shard_map/reshape | solution.py:48
  217.9 8.8 %all-to-all-start.2 = ((bf16[32,64,512]{2,1,0:T(8,128)(2,1)}), bf16[32,64,512]{2,1,0:T(8,128)(2,1)S(1)}, u32[]{:S(2)}, u32[]{:S(2)}) async-start(bf16[32,64,512]{2,1,0:T(8,128)(2,1)} %reshape.131), calls=%async_computation.2 | async-start | bytes 4194304 | tf_op jit(solution)/shard_map/all_to_all | solution.py:103
  226.6 0.6 copy.65
  227.2 0.6 pad_clamp_fusion
  227.8 0.6 iota_compare_fusion.1
  228.4 0.6 convert_bitcast_fusion.5
  229.0 0.6 bitcast_convert_fusion
  229.6 1.3 convert_bitcast_fusion.3
  231.0 2.2 copy.63
  233.2 1.4 fusion.29
  234.7 2.6 multiply_reduce_fusion.3
  237.3 38.1 %all-to-all-done.2 = bf16[32,64,512]{2,1,0:T(8,128)(2,1)S(1)} async-done(((bf16[32,64,512]{2,1,0:T(8,128)(2,1)}), bf16[32,64,512]{2,1,0:T(8,128)(2,1)S(1)}, u32[]{:S(2)}, u32[]{:S(2)}) %all-to-all-start.2) | async-done | bytes 2097184 | tf_op jit(solution)/shard_map/all_to_all | solution.py:103
  275.4 1.7 gather_fusion
  277.1 3.1 multiply_reduce_fusion.1
  280.2 32.7 %all-reduce = (f32[1,128]{1,0:T(1,128)S(1)}, f32[16,64]{1,0:T(8,128)S(1)}) all-reduce(f32[1,128]{1,0:T(1,128)S(1)} %bitcast.190, f32[16,64]{1,0:T(8,128)S(1)} %get-tuple-element.72), channel_id=1, replica_groups=mesh['seq'=32,'head'=16] {'head'}, use_global_device_ids=true, to_apply=%region_2.3 | all-reduce | flops 1152 | bytes 9216 | tf_op jit(solution)/shard_map/psum | solution.py:109
  313.1 0.8 copy.76
  313.9 1.3 copy_bitcast_fusion.2
  (60 shorter events, 2.6 us)
Async XLA Ops:
  0.6 276.4 %copy-start = (bf16[16,64,512]{2,1,0:T(8,128)(2,1)S(1)}, bf16[16,64,512]{2,1,0:T(8,128)(2,1)}, u32[]{:S(2)}) copy-start(bf16[16,64,512]{2,1,0:T(8,128)(2,1)} %param.19) | copy-start | bytes 3145732
  0.6 15.7 %copy-start.3 = (bf16[16,64,512]{2,1,0:T(8,128)(2,1)S(1)}, bf16[16,64,512]{2,1,0:T(8,128)(2,1)}, u32[]{:S(2)}) copy-start(bf16[16,64,512]{2,1,0:T(8,128)(2,1)} %param.17) | copy-start | bytes 3145732
  4.3 19.4 %all-to-all-start.1 = ((bf16[32,2,640]{2,1,0:T(2,128)(2,1)}), bf16[32,2,640]{2,1,0:T(2,128)(2,1)S(1)}, u32[]{:S(2)}, u32[]{:S(2)}) async-start(bf16[32,2,640]{2,1,0:T(2,128)(2,1)} %reshape.168), calls=%async_computation.1 | async-start | bytes 163840 | tf_op jit(solution)/shard_map/all_to_all | solution.py:100
  19.4 9.5 %copy-start.6 = (bf16[128,512]{1,0:T(8,128)(2,1)S(1)}, bf16[128,512]{1,0:T(8,128)(2,1)}, u32[]{:S(2)}) copy-start(bf16[128,512]{1,0:T(8,128)(2,1)} %param.13) | copy-start | bytes 393220
  19.4 9.6 %copy-start.5 = (bf16[128,512]{1,0:T(8,128)(2,1)S(1)}, bf16[128,512]{1,0:T(8,128)(2,1)}, u32[]{:S(2)}) copy-start(bf16[128,512]{1,0:T(8,128)(2,1)} %param.14) | copy-start | bytes 393220
  23.8 107.8 %all-to-all-start = ((bf16[32,64,512]{2,1,0:T(8,128)(2,1)}), bf16[32,64,512]{2,1,0:T(8,128)(2,1)}, u32[]{:S(2)}, u32[]{:S(2)}) async-start(bf16[32,64,512]{2,1,0:T(8,128)(2,1)} %scatter_fusion), calls=%async_computation | async-start | bytes 4194304 | tf_op jit(solution)/shard_map/all_to_all | solution.py:99
  29.2 51.7 %collective-permute-start = (f32[4,128,128]{2,1,0:T(8,128)S(1)}, f32[4,128,128]{2,1,0:T(8,128)S(1)}, u32[]{:S(2)}, u32[]{:S(2)}) collective-permute-start(f32[4,128,128]{2,1,0:T(8,128)S(1)} %fusion.3), channel_id=1, source_target_pairs={{0,16},{16,0},{32,48},{48,32},{64,80},{80,64},{96,112},{112,96},{1... | collective-permute-start | bytes 786440 | tf_op jit(solution)/shard_map/ppermute | solution.py:13
  81.0 16.2 %collective-permute-start.1 = (f32[4,128,128]{2,1,0:T(8,128)S(1)}, f32[4,128,128]{2,1,0:T(8,128)S(1)}, u32[]{:S(2)}, u32[]{:S(2)}) collective-permute-start(f32[4,128,128]{2,1,0:T(8,128)S(1)} %add.42), channel_id=1, source_target_pairs={{0,32},{16,48},{32,0},{48,16},{64,96},{80,112},{96,64},{112,80},{1... | collective-permute-start | bytes 786440 | tf_op jit(solution)/shard_map/ppermute | solution.py:13
  97.2 18.5 %collective-permute-start.2 = (f32[4,128,128]{2,1,0:T(8,128)S(1)}, f32[4,128,128]{2,1,0:T(8,128)S(1)}, u32[]{:S(2)}, u32[]{:S(2)}) collective-permute-start(f32[4,128,128]{2,1,0:T(8,128)S(1)} %add.43), channel_id=1, source_target_pairs={{0,64},{16,80},{32,96},{48,112},{64,0},{80,16},{96,32},{112,48},{1... | collective-permute-start | bytes 786440 | tf_op jit(solution)/shard_map/ppermute | solution.py:13
  115.8 8.1 %collective-permute-start.3 = (f32[4,128,128]{2,1,0:T(8,128)S(1)}, f32[4,128,128]{2,1,0:T(8,128)S(1)}, u32[]{:S(2)}, u32[]{:S(2)}) collective-permute-start(f32[4,128,128]{2,1,0:T(8,128)S(1)} %add.44), channel_id=1, source_target_pairs={{0,128},{16,144},{32,160},{48,176},{64,192},{80,208},{96,224},{112... | collective-permute-start | bytes 786440 | tf_op jit(solution)/shard_map/ppermute | solution.py:13
  123.9 7.2 %collective-permute-start.4 = (bf16[4,128,128]{2,1,0:T(8,128)(2,1)S(1)}, bf16[4,128,128]{2,1,0:T(8,128)(2,1)S(1)}, u32[]{:S(2)}, u32[]{:S(2)}) collective-permute-start(bf16[4,128,128]{2,1,0:T(8,128)(2,1)S(1)} %add.45), channel_id=1, source_target_pairs={{0,256},{16,272},{32,288},{48,304},{64,320},{80,336},{96,352},{112... | collective-permute-start | bytes 393224 | tf_op jit(solution)/shard_map/ppermute | solution.py:13
  131.2 4.3 %copy-start.1 = (bf16[5,4,128,128]{3,2,1,0:T(8,128)(2,1)}, bf16[5,4,128,128]{3,2,1,0:T(8,128)(2,1)S(1)}, u32[]{:S(2)}) copy-start(bf16[5,4,128,128]{3,2,1,0:T(8,128)(2,1)S(1)} %fusion.26) | copy-start | bytes 1966084
  217.8 8.8 %copy-start.11 = (bf16[6,4,128]{2,1,0:T(4,128)(2,1)S(1)}, bf16[6,4,128]{2,1,0:T(4,128)(2,1)}, u32[]{:S(2)}) copy-start(bf16[6,4,128]{2,1,0:T(4,128)(2,1)} %param.15) | copy-start | bytes 18436
  217.8 11.2 %copy-start.13 = (bf16[512]{0:T(512)(128)(2,1)S(1)}, bf16[512]{0:T(512)(128)(2,1)}, u32[]{:S(2)}) copy-start(bf16[512]{0:T(512)(128)(2,1)} %param.16) | copy-start | bytes 3076
  217.8 15.3 %copy-start.4 = (bf16[128,512]{1,0:T(8,128)(2,1)S(1)}, bf16[128,512]{1,0:T(8,128)(2,1)}, u32[]{:S(2)}) copy-start(bf16[128,512]{1,0:T(8,128)(2,1)} %param.12) | copy-start | bytes 393220
  217.9 57.5 %all-to-all-start.2 = ((bf16[32,64,512]{2,1,0:T(8,128)(2,1)}), bf16[32,64,512]{2,1,0:T(8,128)(2,1)S(1)}, u32[]{:S(2)}, u32[]{:S(2)}) async-start(bf16[32,64,512]{2,1,0:T(8,128)(2,1)} %reshape.131), calls=%async_computation.2 | async-start | bytes 4194304 | tf_op jit(solution)/shard_map/all_to_all | solution.py:103
  233.1 1.4 copy-start.7
  237.3 39.8 %copy-start.8 = (f32[16,64,4]{1,2,0:T(4,128)S(1)}, f32[16,64,4]{1,2,0:T(4,128)}, u32[]{:S(2)}) copy-start(f32[16,64,4]{1,2,0:T(4,128)} %convert_bitcast_fusion.3) | copy-start | bytes 49156
  237.3 39.8 %copy-start.10 = (pred[64,64]{1,0:T(8,128)(4,1)S(1)}, pred[64,64]{1,0:T(8,128)(4,1)}, u32[]{:S(2)}) copy-start(pred[64,64]{1,0:T(8,128)(4,1)} %iota_compare_fusion.1) | copy-start | bytes 12292
  277.1 3.1 copy-start.12
  277.1 35.8 %copy-start.2 = (f32[1,128,4,128]{1,3,2,0:T(8,128)S(1)}, f32[1,128,4,128]{1,3,2,0:T(8,128)}, u32[]{:S(2)}) copy-start(f32[1,128,4,128]{1,3,2,0:T(8,128)} %get-tuple-element.71) | copy-start | bytes 786436
  277.1 35.8 %copy-start.9 = (f32[4,128]{1,0:T(4,128)S(1)}, f32[4,128]{1,0:T(4,128)}, u32[]{:S(2)}) copy-start(f32[4,128]{1,0:T(4,128)} %bitcast_convert_fusion) | copy-start | bytes 6148
where the time goes:
time: 317 us; the launch traced here: 315 us
  waiting for transfers between devices  124 us (39%)
  local copies, waits for them, and re-layouts  73 us (23%)
  starting transfers between devices  44.4 us (14%)
  blocking collectives  32.7 us (10%)
  other arithmetic  29.5 us (9%)
  matrix products  10.6 us (3%)
    ppermute x5, waiting for transfers between devices, partner_2(): return lax.ppermute(value, axis, pairs)  81.3 us
    all_to_all x1, waiting for transfers between devices, local(): lax.all_to_all(answers, 'seq', split_axis=0, concat_axis=0, tiled=True)  38.1 us
    psum x1, blocking collectives, local(): slab_square, user_square = lax.psum((slab_square, user_square), 'head')  32.7 us
    reshape x4, local copies, waits for them, and re-layouts, read_prefix(): projected = projected.reshape(projected.shape[:3] + (level_count, outer))  29.4 us
    reduce_sum x5, other arithmetic, read_prefix(): return jnp.sum(projected * scale_rows, axis=3)  22.8 us
    ppermute x5, starting transfers between devices, partner_2(): return lax.ppermute(value, axis, pairs)  20 us
    transpose x4, local copies, waits for them, and re-layouts, read_prefix(): jnp.einsum('bthd,hdf->bthf', query_rows, merged, preferred_element_type=j...  11 us
    all_to_all x1, starting transfers between devices, local(): lax.all_to_all(send_weights, 'seq', split_axis=0, concat_axis=0, tiled=True)  10.5 us
  transfers between devices with their start and end apart: 8, of which 7 were waited for; matrix products, arithmetic and copies ran while one was open for 5% of the time, Pallas kernels for 0%

commit v1 on v0

v1 whole, which is shorter than its diff:
```python
import functools
import heapq

import jax
import jax.numpy as jnp
from jax import lax
from jax.experimental import pallas as pl
from jax.experimental.pallas import tpu as pltpu
from jax.sharding import PartitionSpec as P

HEADS = 64
HD = 128
MESH = pl.DeviceIdType.MESH
F32 = jnp.float32
BF16 = jnp.bfloat16

UNITS = (
    (0, 128, "A", 0, 0),
    (128, 128, "A", 2, 1),
    (256, 64, "A", 3, 0),
    (320, 64, "B", 3, 1),
    (384, 128, "B", 1, 0),
)
HEAD_UNITS = ((0,), (1,), (2, 3), (4,))
LINK_KB_PER_US = 46.5
HOP_US = 1.7
ISSUE_AHEAD_US = 2.0
PIECE_US = 0.6


def reach(ring, plus):
    return (ring // 2, (ring - 1) // 2) if plus else ((ring - 1) // 2, ring // 2)


def forwards(nx, ny, unit, ex, ey):
    _, _, route, _, parity = UNITS[unit]
    result = []

    def along_x(plus):
        ahead, back = reach(nx, plus)
        if 0 <= ex < ahead:
            result.append(("x+", ex + 1, ey))
        if 0 <= -ex < back:
            result.append(("x-", ex - 1, ey))

    def along_y(plus):
        ahead, back = reach(ny, plus)
        if 0 <= ey < ahead:
            result.append(("y+", ex, ey + 1))
        if 0 <= -ey < back:
            result.append(("y-", ex, ey - 1))

    if route == "A":
        if ex == 0:
            along_y(parity % 2 == 0)
        along_x((parity + ey) % 2 == 0)
    else:
        if ey == 0:
            along_x(parity % 2 == 0)
        along_y((parity + ex) % 2 == 0)
    return result


def gather_order(nx, ny):
    def depth(unit, ex, ey):
        return max([1 + depth(unit, a, b) for _, a, b in forwards(nx, ny, unit, ex, ey)], default=0)

    waiting = {link: [] for link in ("x+", "x-", "y+", "y-")}
    free = dict.fromkeys(waiting, 0.0)
    arrival = {(unit, 0, 0): 0.0 for unit in range(len(UNITS))}
    events = [(0.0, unit, 0, 0) for unit in range(len(UNITS))]
    heapq.heapify(events)
    sends, now = [], 0.0
    while True:
        while events and events[0][0] <= now + 1e-9:
            time, unit, ex, ey = heapq.heappop(events)
            for link, a, b in forwards(nx, ny, unit, ex, ey):
                entry = (UNITS[unit][3], -depth(unit, a, b), time, unit, ex, ey, a, b)
                heapq.heappush(waiting[link], entry)
        for link, queue in waiting.items():
            if queue and free[link] <= now + 1e-9:
                _, _, time, unit, ex, ey, a, b = heapq.heappop(queue)
                free[link] = now + UNITS[unit][1] * 0.25 / LINK_KB_PER_US
                sends.append((max(time, now - ISSUE_AHEAD_US), len(sends), link, unit, (ex, ey), (a, b)))
                arrival[(unit, a, b)] = free[link] + HOP_US
                heapq.heappush(events, (arrival[(unit, a, b)], unit, a, b))
        later = [event[0] for event in events[:1]]
        later += [free[link] for link, queue in waiting.items() if queue]
        later = [time for time in later if time > now]
        if not later:
            return sorted(sends), arrival
        now = min(later)


def kernel(
    n_seq,
    n_head,
    prefix_hbm,
    slab_q,
    slab_k,
    slab_v,
    slab_w,
    gain_hbm,
    user_q,
    user_k,
    user_v,
    user_w,
    slab_out,
    user_out,
    prefix_ref,
    q_buf,
    k_buf,
    v_buf,
    slab_w_buf,
    user_w_buf,
    gain_buf,
    blocks,
    nodes,
    scaled,
    total,
    staged,
    square_send,
    square_recv,
    root_buf,
    in_sem,
    out_sem,
    send_sem,
    recv_sem,
    head_send_sem,
    head_recv_sem,
):
    pairs = user_q.shape[0]
    heads = q_buf.shape[2] // HD
    suffix = q_buf.shape[1] // 2
    rows = 2 * suffix
    depth = n_seq.bit_length() - 1
    nx = 1 << (depth // 2)
    ny = n_seq // nx
    me = lax.axis_index("seq")
    me_head = lax.axis_index("head")
    x, y = me // ny, lax.rem(me, ny)

    def block_at(dx, dy):
        return lax.rem(x + (dx + nx), nx) * ny + lax.rem(y + (dy + ny), ny)

    loads = [
        pltpu.make_async_copy(source, target, in_sem.at[index])
        for index, (source, target) in enumerate(
            (
                (slab_k, k_buf.at[pairs]),
                (slab_v, v_buf.at[pairs]),
                (slab_q, q_buf.at[pairs]),
                (slab_w, slab_w_buf),
                (prefix_hbm, prefix_ref),
                (user_w, user_w_buf),
                (user_q, q_buf.at[pl.ds(0, pairs)]),
                (user_k, k_buf.at[pl.ds(0, pairs)]),
                (user_v, v_buf.at[pl.ds(0, pairs)]),
                (gain_hbm, gain_buf),
            )
        )
    ]
    for load in loads:
        load.start()

    neighbours = {
        "x+": block_at(1, 0),
        "x-": block_at(-1, 0),
        "y+": block_at(0, 1),
        "y-": block_at(0, -1),
    }
    barrier = pltpu.get_barrier_semaphore()
    for step in range(1, n_head):
        pl.semaphore_signal(
            barrier,
            inc=1,
            device_id=(me, lax.rem(me_head + step, n_head)),
            device_id_type=MESH,
        )
    for link in neighbours:
        pl.semaphore_signal(
            barrier, inc=1, device_id=(neighbours[link], me_head), device_id_type=MESH
        )

    loads[0].wait()
    loads[1].wait()
    for head in range(heads):
        lanes = slice(head * HD, (head + 1) * HD)
        state = lax.dot_general(
            k_buf[pairs, :, lanes],
            v_buf[pairs, :, lanes],
            (((0,), (0,)), ((), ())),
            preferred_element_type=F32,
        )
        blocks[me, lanes, :] = state.astype(BF16)
    pl.semaphore_wait(barrier, n_head - 1 + len(neighbours))

    sends, arrival = gather_order(nx, ny)
    slots = {key: index for index, key in enumerate(sorted(arrival))}

    def piece_copy(key, slot, link):
        unit, ex, ey = key
        piece = blocks.at[block_at(-ex, -ey), pl.ds(UNITS[unit][0], UNITS[unit][1])]
        return pltpu.make_async_remote_copy(
            src_ref=piece,
            dst_ref=piece,
            send_sem=send_sem.at[slot],
            recv_sem=recv_sem.at[slot],
            device_id=(neighbours[link], me_head),
            device_id_type=MESH,
        )

    arrived = {(unit, 0, 0) for unit in range(len(UNITS))}

    def await_piece(key):
        if key not in arrived:
            arrived.add(key)
            piece_copy(key, slots[key], "x+").wait_recv()

    row_ids = lax.broadcasted_iota(jnp.int32, (rows, rows), 0)
    col_ids = lax.broadcasted_iota(jnp.int32, (rows, rows), 1)
    causal = col_ids <= row_ids
    same_user = (row_ids // suffix) == (col_ids // suffix)
    spread = (
        lax.broadcasted_iota(jnp.int32, (heads, heads * HD), 0)
        == lax.broadcasted_iota(jnp.int32, (heads, heads * HD), 1) // HD
    ).astype(BF16)

    def widen(weights):
        return lax.dot_general(
            weights, spread, (((0,), (0,)), ((), ())), preferred_element_type=F32
        )

    def scale_rows(pair, first, count, weights_at, position):
        queries = q_buf[pair, pl.ds(first, count), :].astype(F32)
        for level in range(1, depth + 1):
            bit = lax.rem(position >> (level - 1), 2).astype(F32)
            product = (queries * (widen(weights_at(level)) * bit)).astype(BF16)
            for head in range(heads):
                scaled[pair, head, pl.ds(first, count), (level - 1) * HD : level * HD] = product[
                    :, head * HD : (head + 1) * HD
                ]

    def scale_piece(pair):
        if pair == pairs:
            scale_rows(pair, 0, rows, lambda level: slab_w_buf[level], me)
        else:
            for half in range(2):
                user = 2 * pair + half
                scale_rows(
                    pair,
                    half * suffix,
                    suffix,
                    lambda level: user_w_buf[user, level],
                    prefix_ref[user],
                )

    def local_piece(pair):
        if pair == pairs:
            weights = widen(slab_w_buf[0])
            mask = causal
        else:
            weights = jnp.concatenate(
                [widen(user_w_buf[2 * pair + half, 0]) for half in range(2)], axis=0
            )
            mask = jnp.logical_and(causal, same_user)
        for head in range(heads):
            lanes = slice(head * HD, (head + 1) * HD)
            scores = lax.dot_general(
                q_buf[pair, :, lanes],
                k_buf[pair, :, lanes],
                (((1,), (1,)), ((), ())),
                preferred_element_type=F32,
            )
            scores = jnp.where(mask, scores, 0.0).astype(BF16)
            result = jnp.dot(scores, v_buf[pair, :, lanes], preferred_element_type=F32)
            total[pair, :, lanes] = result * weights[:, lanes]

    first_node = [0]
    for level in range(1, depth + 1):
        first_node.append(first_node[-1] + (n_seq >> level))

    def build_nodes(head):
        chunk = 16

        @pl.loop(0, HD // chunk)
        def _(part):
            start = pl.multiple_of(part * chunk, chunk)
            source = pl.ds(pl.multiple_of(head * HD + part * chunk, chunk), chunk)

            def tree(level, index):
                if level == 0:
                    value = blocks[index, source, :]
                    if index % 2 == 0:
                        nodes[head, first_node[0] + index // 2, pl.ds(start, chunk), :] = value
                    return value.astype(F32)
                value = tree(level - 1, 2 * index) + tree(level - 1, 2 * index + 1)
                if level < depth and index % 2 == 0:
                    nodes[head, first_node[level] + index // 2, pl.ds(start, chunk), :] = (
                        value.astype(BF16)
                    )
                return value

            tree(depth - 1, 0)
            rest = 1
            for level in range(depth - 2, -1, -1):
                rest = 2 * rest
                tree(level, rest)
                rest = rest + 1

    def read_rows(pair, head, first, count, position):
        states = jnp.concatenate(
            [
                nodes[head, first_node[level - 1] + (position >> level)]
                for level in range(1, depth + 1)
            ],
            axis=0,
        )
        return jnp.dot(
            scaled[pair, head, pl.ds(first, count), :], states, preferred_element_type=F32
        )

    def read_pair(pair, head):
        lanes = slice(head * HD, (head + 1) * HD)
        if pair is None:
            total[pairs, :, lanes] += read_rows(pairs, head, 0, rows, me)
        else:
            for half in range(2):
                first = half * suffix
                total[pair, pl.ds(first, suffix), lanes] += read_rows(
                    pair, head, first, suffix, prefix_ref[2 * pair + half]
                )

    def read_head(head):
        for unit in HEAD_UNITS[head]:
            for key in sorted(arrival):
                if key[0] == unit:
                    await_piece(key)
        build_nodes(head)
        read_pair(None, head)

        @pl.loop(0, pairs)
        def _(pair):
            read_pair(pair, head)

    timeline = [(time, 0, index, "send", index) for index, (time, *_) in enumerate(sends)]
    pieces = []
    for step in range(pairs + 1):
        pair = pairs - step
        pieces += [(scale_piece, pair), (local_piece, pair)]
    last_load = {pairs: 4}
    for index, piece in enumerate(pieces):
        timeline.append((0.3 + PIECE_US * index, 1, index, "piece", piece))
    work_end = 0.3 + PIECE_US * len(pieces)
    for head in range(heads):
        done = max(
            time for key, time in arrival.items() if key[0] in HEAD_UNITS[head]
        )
        timeline.append((max(done, work_end) + 0.1, 2, head, "head", head))
    loads_waited = 2
    copies = []
    for _, _, _, kind, item in sorted(timeline, key=lambda entry: entry[:3]):
        if kind == "send":
            _, _, link, unit, (ex, ey), (a, b) = sends[item]
            await_piece((unit, ex, ey))
            source = blocks.at[block_at(-ex, -ey), pl.ds(UNITS[unit][0], UNITS[unit][1])]
            slot = slots[(unit, a, b)]
            copy = pltpu.make_async_remote_copy(
                src_ref=source,
                dst_ref=source,
                send_sem=send_sem.at[slot],
                recv_sem=recv_sem.at[slot],
                device_id=(neighbours[link], me_head),
                device_id_type=MESH,
            )
            copy.start()
            copies.append(copy)
        elif kind == "piece":
            work, pair = item
            needed = last_load.get(pair, 9)
            while loads_waited < needed:
                loads[loads_waited].wait()
                loads_waited += 1
            work(pair)
        else:
            read_head(item)
    loads[9].wait()

    lane_ids = lax.broadcasted_iota(jnp.int32, (rows, HD), 1)
    squares = jnp.zeros((rows, HD), F32)
    for pair in range(pairs + 1):
        values = total[pair]
        values = values * values
        column = jnp.sum(values, axis=1, keepdims=True)
        squares = jnp.where(lane_ids == pair, column, squares)
    kept = square_send.shape[0]
    square_send[...] = squares.T[:kept]
    head_copies = []
    for step in sorted(range(1, n_head), key=lambda s: -min(s, n_head - s)):
        copy = pltpu.make_async_remote_copy(
            src_ref=square_send,
            dst_ref=square_recv.at[step],
            send_sem=head_send_sem.at[step],
            recv_sem=head_recv_sem.at[step],
            device_id=(me, lax.rem(me_head + step, n_head)),
            device_id_type=MESH,
        )
        copy.start()
        head_copies.append((step, copy))
    summed = square_send[...]
    for step, copy in reversed(head_copies):
        copy.wait_recv()
        summed = summed + square_recv[step]
    inverse = 1.0 / jnp.sqrt(summed * (1.0 / (HEADS * HD)) + 1e-6)
    root_buf[...] = jnp.concatenate([inverse, jnp.zeros((HD - kept, rows), F32)], axis=0).T

    gain = gain_buf[...].astype(F32).reshape(1, heads * HD)
    outs = []
    for pair in range(pairs, -1, -1):
        scale = root_buf[:, pair : pair + 1]
        staged[pair] = (total[pair] * scale * gain).astype(BF16)
        target = slab_out if pair == pairs else user_out.at[pair]
        out = pltpu.make_async_copy(staged.at[pair], target, out_sem.at[pair])
        out.start()
        outs.append(out)
    for copy in copies:
        copy.wait_send()
    for _, copy in head_copies:
        copy.wait_send()
    for out in outs:
        out.wait()


def local(
    slab_query,
    slab_key,
    slab_value,
    slab_levels,
    norm_gain,
    user_query,
    user_key,
    user_value,
    user_levels,
    prefix_lengths,
):
    n_seq, n_head = lax.axis_size("seq"), lax.axis_size("head")
    tokens, width = slab_query.shape
    users, suffix = user_query.shape[:2]
    heads = width // HD
    pairs = users // 2
    depth = n_seq.bit_length() - 1
    paired = (pairs, 2 * suffix, width)
    whole = pl.BlockSpec(memory_space=pl.ANY)
    slot_count = n_seq * len(UNITS)
    buffers = (pairs + 1, tokens, width)
    kept = -(-(pairs + 1) // 8) * 8
    slab_out, user_out = pl.pallas_call(
        functools.partial(kernel, n_seq, n_head),
        out_shape=(
            jax.ShapeDtypeStruct((tokens, width), BF16),
            jax.ShapeDtypeStruct(paired, BF16),
        ),
        in_specs=[whole] * 10,
        out_specs=(whole, whole),
        scratch_shapes=[
            pltpu.SMEM(prefix_lengths.shape, jnp.int32),
            pltpu.VMEM(buffers, BF16),
            pltpu.VMEM(buffers, BF16),
            pltpu.VMEM(buffers, BF16),
            pltpu.VMEM(slab_levels.shape, BF16),
            pltpu.VMEM(user_levels.shape, BF16),
            pltpu.VMEM(norm_gain.shape, BF16),
            pltpu.VMEM((n_seq, width, HD), BF16),
            pltpu.VMEM((heads, n_seq - 1, HD, HD), BF16),
            pltpu.VMEM((pairs + 1, heads, tokens, depth * HD), BF16),
            pltpu.VMEM(buffers, F32),
            pltpu.VMEM(buffers, BF16),
            pltpu.VMEM((kept, tokens), F32),
            pltpu.VMEM((n_head, kept, tokens), F32),
            pltpu.VMEM((tokens, HD), F32),
            pltpu.SemaphoreType.DMA((10,)),
            pltpu.SemaphoreType.DMA((pairs + 1,)),
            pltpu.SemaphoreType.DMA((slot_count,)),
            pltpu.SemaphoreType.DMA((slot_count,)),
            pltpu.SemaphoreType.DMA((n_head,)),
            pltpu.SemaphoreType.DMA((n_head,)),
        ],
        compiler_params=pltpu.CompilerParams(
            collective_id=0, has_side_effects=True, vmem_limit_bytes=50 * 1024 * 1024
        ),
    )(
        *(
            pltpu.with_memory_space_constraint(array, pltpu.HBM)
            for array in (
                prefix_lengths,
                slab_query,
                slab_key,
                slab_value,
                slab_levels,
                norm_gain,
                user_query.reshape(paired),
                user_key.reshape(paired),
                user_value.reshape(paired),
                user_levels,
            )
        ),
    )
    return slab_out, user_out.reshape(user_query.shape)


def solution(mesh):
    return jax.shard_map(
        local,
        mesh=mesh,
        in_specs=(
            P("seq", "head"),
            P("seq", "head"),
            P("seq", "head"),
            P(None, "head", "seq"),
            P("head"),
            P("seq", None, "head"),
            P("seq", None, "head"),
            P("seq", None, "head"),
            P("seq", None, "head", None),
            P("seq"),
        ),
        out_specs=(P("seq", "head"), P("seq", None, "head")),
        check_vma=False,
    )
```

time: 317 us -> 65.8 us (0.21)
  waiting for transfers between devices: 124 us -> 0 us
  local copies, waits for them, and re-layouts: 73 us -> 1.63 us
  Pallas kernels: 0 us -> 63.4 us
  starting transfers between devices: 44.4 us -> 0 us
  blocking collectives: 32.7 us -> 0 us
  other arithmetic: 29.5 us -> 0 us
  matrix products: 10.6 us -> 0 us
    ppermute x5 -> x0, waiting for transfers between devices: 81.3 us -> none  [partner_2(): return lax.ppermute(value, axis, pairs)]
    pallas_call x0 -> x1, Pallas kernels: none -> 63.4 us  [local(): pl.pallas_call(functools.partial(kernel, n_seq, n_head), out_shape=(jax.S...]
    all_to_all x3 -> x0, waiting for transfers between devices: 42.4 us -> none  [the longest x1 38.1 us: local(): lax.all_to_all(answers, 'seq', split_axis=0, concat_axis=0, tiled=True)]
    reshape x6 -> x0, local copies, waits for them, and re-layouts: 37.5 us -> none  [the longest x4 29.4 us: read_prefix(): projected = projected.reshape(projected.shape[:3] + (level_count, outer))]
    psum x1 -> x0, blocking collectives: 32.7 us -> none  [local(): slab_square, user_square = lax.psum((slab_square, user_square), 'head')]
    all_to_all x3 -> x0, starting transfers between devices: 24.4 us -> none  [the longest x1 10.5 us: local(): lax.all_to_all(send_weights, 'seq', split_axis=0, concat_axis=0, tiled=True)]
    reduce_sum x5 -> x0, other arithmetic: 22.8 us -> none  [read_prefix(): return jnp.sum(projected * scale_rows, axis=3)]
    ppermute x5 -> x0, starting transfers between devices: 20 us -> none  [partner_2(): return lax.ppermute(value, axis, pairs)]
  transfers between devices with their start and end apart: 8 -> 0, of which waited for: 7 -> 0; matrix products, arithmetic and copies ran while one was open for 5% -> 0% of each run, Pallas kernels for 0% -> 0%
where the time goes in v1:
time: 65.8 us; the launch traced here: 65.6 us
  Pallas kernels  63.4 us (96%)
  local copies, waits for them, and re-layouts  1.63 us (2%)
    pallas_call x1, Pallas kernels, local(): pl.pallas_call(functools.partial(kernel, n_seq, n_head), out_shape=(jax.S...  63.4 us
    unnamed x2, local copies, waits for them, and re-layouts  1.63 us

profile of v1, /device:TPU:1, one launch (start us, length us, event | category | flops | bytes accessed | tf_op | source)
XLA Modules:
  0.0 65.6 jit_solution(15697824218530821658)
XLA Ops:
  0.6 63.4 %shard_map.113 = (bf16[128,512]{1,0:T(8,128)(2,1)S(1)}, bf16[8,128,512]{2,1,0:T(8,128)(2,1)S(1)}) custom-call(s32[16]{0:T(128)} %prefix_hbm.1, bf16[128,512]{1,0:T(8,128)(2,1)} %slab_q.1, bf16[128,512]{1,0:T(8,128)(2,1)} %slab_k.1, bf16[128,512]{1,0:T(8,128)(2,1)} %slab_v.1, bf16[6,4,128]{2,1,0:T(4,128)(2,1)} %slab_w.1, bf16[512]{0:T(512)(128)(2,1)} %gain_hbm.1, ...), custom_call_target="tpu_custom_call" | custom-call | tf_op jit(solution)/shard_map/pallas_call | solution.py:457
  64.0 0.7 %copy.14 = bf16[128,512]{1,0:T(8,128)(2,1)} copy(bf16[128,512]{1,0:T(8,128)(2,1)S(1)} %get-tuple-element.8) | data formatting | bytes 262144
  64.7 1.0 %copy.15 = bf16[16,64,512]{2,1,0:T(8,128)(2,1)} copy(bf16[16,64,512]{2,1,0:T(8,128)(2,1)S(1)} %bitcast.4) | data formatting | bytes 2097152

commit v2 on v1

--- a/solution.py
+++ b/solution.py
@@ -17,15 +17,17 @@
 UNITS = (
     (0, 128, "A", 0, 0),
     (128, 128, "A", 2, 1),
-    (256, 64, "A", 3, 0),
-    (320, 64, "B", 3, 1),
+    (256, 48, "A", 3, 0),
+    (304, 80, "B", 3, 1),
     (384, 128, "B", 1, 0),
 )
 HEAD_UNITS = ((0,), (1,), (2, 3), (4,))
+LINKS = ("x+", "x-", "y+", "y-")
 LINK_KB_PER_US = 46.5
-HOP_US = 1.7
-ISSUE_AHEAD_US = 2.0
-PIECE_US = 0.6
+HOP_US = 2.6
+ISSUE_AHEAD_US = 0.5
+PRIORITY_WEIGHT = 0.3
+WORK_US = 0.4
 
 
 def reach(ring, plus):
@@ -61,35 +63,55 @@
     return result
 
 
-def gather_order(nx, ny):
-    def depth(unit, ex, ey):
-        return max([1 + depth(unit, a, b) for _, a, b in forwards(nx, ny, unit, ex, ey)], default=0)
-
-    waiting = {link: [] for link in ("x+", "x-", "y+", "y-")}
-    free = dict.fromkeys(waiting, 0.0)
-    arrival = {(unit, 0, 0): 0.0 for unit in range(len(UNITS))}
-    events = [(0.0, unit, 0, 0) for unit in range(len(UNITS))]
-    heapq.heapify(events)
+def plan_gather(nx, ny, work_count):
+    def depth(key):
+        return max([1 + depth((key[0], a, b)) for _, a, b in forwards(nx, ny, *key)], default=0)
+
+    def send_us(unit):
+        return UNITS[unit][1] * 0.25 / LINK_KB_PER_US
+
+    own = [(unit, 0, 0) for unit in range(len(UNITS))]
+    waiting = {link: [] for link in LINKS}
+    free = dict.fromkeys(LINKS, 0.0)
+    events = [(0.0, key) for key in own]
     sends, now = [], 0.0
     while True:
         while events and events[0][0] <= now + 1e-9:
-            time, unit, ex, ey = heapq.heappop(events)
-            for link, a, b in forwards(nx, ny, unit, ex, ey):
-                entry = (UNITS[unit][3], -depth(unit, a, b), time, unit, ex, ey, a, b)
-                heapq.heappush(waiting[link], entry)
+            time, key = heapq.heappop(events)
+            for link, a, b in forwards(nx, ny, *key):
+                target = (key[0], a, b)
+                rank = UNITS[key[0]][3] * PRIORITY_WEIGHT - depth(target)
+                heapq.heappush(waiting[link], (rank, time, key, target))
         for link, queue in waiting.items():
             if queue and free[link] <= now + 1e-9:
-                _, _, time, unit, ex, ey, a, b = heapq.heappop(queue)
-                free[link] = now + UNITS[unit][1] * 0.25 / LINK_KB_PER_US
-                sends.append((max(time, now - ISSUE_AHEAD_US), len(sends), link, unit, (ex, ey), (a, b)))
-                arrival[(unit, a, b)] = free[link] + HOP_US
-                heapq.heappush(events, (arrival[(unit, a, b)], unit, a, b))
+                _, time, key, target = heapq.heappop(queue)
+                free[link] = now + send_us(key[0])
+                heapq.heappush(events, (free[link] + HOP_US, target))
+                sends.append((max(time, now - ISSUE_AHEAD_US), now, link, key, target))
         later = [event[0] for event in events[:1]]
         later += [free[link] for link, queue in waiting.items() if queue]
-        later = [time for time in later if time > now]
+        later = [time for time in later if time > now + 1e-9]
         if not later:
-            return sorted(sends), arrival
+            break
         now = min(later)
+
+    arrival = dict.fromkeys(own, 0.0)
+    free = dict.fromkeys(LINKS, 0.0)
+    steps, now, work = [], 0.0, 0
+    for _, _, link, key, target in sorted(sends):
+        while work < work_count and arrival[key] - now > 0.6 * WORK_US:
+            steps.append(("work", work))
+            work, now = work + 1, now + WORK_US
+        now = max(now, arrival[key])
+        free[link] = max(now, free[link]) + send_us(key[0])
+        arrival[target] = free[link] + HOP_US
+        steps.append(("send", (link, key, target)))
+    steps += [("work", index) for index in range(work, work_count)]
+    complete = [
+        max(time for key, time in arrival.items() if key[0] in units) for units in HEAD_UNITS
+    ]
+    order = sorted(range(len(HEAD_UNITS)), key=lambda head: complete[head])
+    return steps, order, sorted(arrival)
 
 
 def kernel(
@@ -118,19 +140,17 @@
     nodes,
     scaled,
     total,
-    staged,
     square_send,
     square_recv,
-    root_buf,
     in_sem,
-    out_sem,
     send_sem,
     recv_sem,
     head_send_sem,
     head_recv_sem,
 ):
     pairs = user_q.shape[0]
-    heads = q_buf.shape[2] // HD
+    width = q_buf.shape[2]
+    heads = width // HD
     suffix = q_buf.shape[1] // 2
     rows = 2 * suffix
     depth = n_seq.bit_length() - 1
@@ -160,7 +180,7 @@
             )
         )
     ]
-    for load in loads:
+    for load in loads[:2]:
         load.start()
 
     neighbours = {
@@ -192,30 +212,39 @@
             (((0,), (0,)), ((), ())),
             preferred_element_type=F32,
         )
-        blocks[me, lanes, :] = state.astype(BF16)
+        blocks[pl.ds(pl.multiple_of(me * width + head * HD, HD), HD), :] = state.astype(BF16)
+    for load in loads[2:]:
+        load.start()
     pl.semaphore_wait(barrier, n_head - 1 + len(neighbours))
 
-    sends, arrival = gather_order(nx, ny)
-    slots = {key: index for index, key in enumerate(sorted(arrival))}
-
-    def piece_copy(key, slot, link):
+    steps, head_order, pieces = plan_gather(nx, ny, 3 * (pairs + 1))
+    relayed = [key for key in pieces if key[1:] != (0, 0) and forwards(nx, ny, *key)]
+    kept_pieces = [key for key in pieces if not forwards(nx, ny, *key)]
+    slots = {key: index for index, key in enumerate(relayed)}
+
+    def piece_copy(link, key, target):
         unit, ex, ey = key
-        piece = blocks.at[block_at(-ex, -ey), pl.ds(UNITS[unit][0], UNITS[unit][1])]
+        start = pl.multiple_of(block_at(-ex, -ey) * width + UNITS[unit][0], 16)
+        piece = blocks.at[pl.ds(start, UNITS[unit][1])]
         return pltpu.make_async_remote_copy(
             src_ref=piece,
             dst_ref=piece,
-            send_sem=send_sem.at[slot],
-            recv_sem=recv_sem.at[slot],
+            send_sem=send_sem.at[LINKS.index(link)],
+            recv_sem=recv_sem.at[slots.get(target, len(slots) + unit)],
             device_id=(neighbours[link], me_head),
             device_id_type=MESH,
         )
 
-    arrived = {(unit, 0, 0) for unit in range(len(UNITS))}
+    def rows_copy(count, sem):
+        rows_ref = blocks.at[pl.ds(0, count)]
+        return pltpu.make_async_copy(rows_ref, rows_ref, sem)
+
+    waited = set()
 
     def await_piece(key):
-        if key not in arrived:
-            arrived.add(key)
-            piece_copy(key, slots[key], "x+").wait_recv()
+        if key in slots and key not in waited:
+            waited.add(key)
+            piece_copy("x+", key, key).wait_recv()
 
     row_ids = lax.broadcasted_iota(jnp.int32, (rows, rows), 0)
     col_ids = lax.broadcasted_iota(jnp.int32, (rows, rows), 1)
@@ -226,16 +255,16 @@
         == lax.broadcasted_iota(jnp.int32, (heads, heads * HD), 1) // HD
     ).astype(BF16)
 
-    def widen(weights):
+    def widen(weights, lanes_of):
         return lax.dot_general(
-            weights, spread, (((0,), (0,)), ((), ())), preferred_element_type=F32
+            weights, lanes_of, (((0,), (0,)), ((), ())), preferred_element_type=F32
         )
 
     def scale_rows(pair, first, count, weights_at, position):
         queries = q_buf[pair, pl.ds(first, count), :].astype(F32)
         for level in range(1, depth + 1):
             bit = lax.rem(position >> (level - 1), 2).astype(F32)
-            product = (queries * (widen(weights_at(level)) * bit)).astype(BF16)
+            product = (queries * (widen(weights_at(level), spread) * bit)).astype(BF16)
             for head in range(heads):
                 scaled[pair, head, pl.ds(first, count), (level - 1) * HD : level * HD] = product[
                     :, head * HD : (head + 1) * HD
@@ -255,16 +284,21 @@
                     prefix_ref[user],
                 )
 
-    def local_piece(pair):
+    def local_piece(pair, group):
+        group_lanes = slice(group[0] * HD, (group[-1] + 1) * HD)
         if pair == pairs:
-            weights = widen(slab_w_buf[0])
+            weights = widen(slab_w_buf[0], spread[:, group_lanes])
             mask = causal
         else:
             weights = jnp.concatenate(
-                [widen(user_w_buf[2 * pair + half, 0]) for half in range(2)], axis=0
+                [
+                    widen(user_w_buf[2 * pair + half, 0], spread[:, group_lanes])
+                    for half in range(2)
+                ],
+                axis=0,
             )
             mask = jnp.logical_and(causal, same_user)
-        for head in range(heads):
+        for index, head in enumerate(group):
             lanes = slice(head * HD, (head + 1) * HD)
             scores = lax.dot_general(
                 q_buf[pair, :, lanes],
@@ -274,7 +308,7 @@
             )
             scores = jnp.where(mask, scores, 0.0).astype(BF16)
             result = jnp.dot(scores, v_buf[pair, :, lanes], preferred_element_type=F32)
-            total[pair, :, lanes] = result * weights[:, lanes]
+            total[pair, :, lanes] = result * weights[:, index * HD : (index + 1) * HD]
 
     first_node = [0]
     for level in range(1, depth + 1):
@@ -286,11 +320,11 @@
         @pl.loop(0, HD // chunk)
         def _(part):
             start = pl.multiple_of(part * chunk, chunk)
-            source = pl.ds(pl.multiple_of(head * HD + part * chunk, chunk), chunk)
 
             def tree(level, index):
                 if level == 0:
-                    value = blocks[index, source, :]
+                    first = pl.multiple_of(index * width + head * HD + start, chunk)
+                    value = blocks[pl.ds(first, chunk), :]
                     if index % 2 == 0:
                         nodes[head, first_node[0] + index // 2, pl.ds(start, chunk), :] = value
                     return value.astype(F32)
@@ -331,60 +365,36 @@
                     pair, head, first, suffix, prefix_ref[2 * pair + half]
                 )
 
-    def read_head(head):
+    work_items = []
+    for pair in range(pairs, -1, -1):
+        work_items.append(functools.partial(scale_piece, pair))
+        for group in (range(heads // 2), range(heads // 2, heads)):
+            work_items.append(functools.partial(local_piece, pair, group))
+
+    loaded = False
+    sent_rows = dict.fromkeys(LINKS, 0)
+    for kind, item in steps:
+        if kind == "work":
+            for load in () if loaded else loads[2:]:
+                load.wait()
+            loaded = True
+            work_items[item]()
+        else:
+            link, key, target = item
+            await_piece(key)
+            piece_copy(link, key, target).start()
+            sent_rows[link] += UNITS[key[0]][1]
+    for head in head_order:
         for unit in HEAD_UNITS[head]:
-            for key in sorted(arrival):
+            for key in relayed:
                 if key[0] == unit:
                     await_piece(key)
+            kept_rows = UNITS[unit][1] * sum(key[0] == unit for key in kept_pieces)
+            rows_copy(kept_rows, recv_sem.at[len(slots) + unit]).wait()
         build_nodes(head)
         read_pair(None, head)
-
-        @pl.loop(0, pairs)
-        def _(pair):
+        for pair in range(pairs):
             read_pair(pair, head)
-
-    timeline = [(time, 0, index, "send", index) for index, (time, *_) in enumerate(sends)]
-    pieces = []
-    for step in range(pairs + 1):
-        pair = pairs - step
-        pieces += [(scale_piece, pair), (local_piece, pair)]
-    last_load = {pairs: 4}
-    for index, piece in enumerate(pieces):
-        timeline.append((0.3 + PIECE_US * index, 1, index, "piece", piece))
-    work_end = 0.3 + PIECE_US * len(pieces)
-    for head in range(heads):
-        done = max(
-            time for key, time in arrival.items() if key[0] in HEAD_UNITS[head]
-        )
-        timeline.append((max(done, work_end) + 0.1, 2, head, "head", head))
-    loads_waited = 2
-    copies = []
-    for _, _, _, kind, item in sorted(timeline, key=lambda entry: entry[:3]):
-        if kind == "send":
-            _, _, link, unit, (ex, ey), (a, b) = sends[item]
-            await_piece((unit, ex, ey))
-            source = blocks.at[block_at(-ex, -ey), pl.ds(UNITS[unit][0], UNITS[unit][1])]
-            slot = slots[(unit, a, b)]
-            copy = pltpu.make_async_remote_copy(
-                src_ref=source,
-                dst_ref=source,
-                send_sem=send_sem.at[slot],
-                recv_sem=recv_sem.at[slot],
-                device_id=(neighbours[link], me_head),
-                device_id_type=MESH,
-            )
-            copy.start()
-            copies.append(copy)
-        elif kind == "piece":
-            work, pair = item
-            needed = last_load.get(pair, 9)
-            while loads_waited < needed:
-                loads[loads_waited].wait()
-                loads_waited += 1
-            work(pair)
-        else:
-            read_head(item)
-    loads[9].wait()
 
     lane_ids = lax.broadcasted_iota(jnp.int32, (rows, HD), 1)
     squares = jnp.zeros((rows, HD), F32)
@@ -395,40 +405,34 @@
         squares = jnp.where(lane_ids == pair, column, squares)
     kept = square_send.shape[0]
     square_send[...] = squares.T[:kept]
-    head_copies = []
     for step in sorted(range(1, n_head), key=lambda s: -min(s, n_head - s)):
-        copy = pltpu.make_async_remote_copy(
-            src_ref=square_send,
-            dst_ref=square_recv.at[step],
-            send_sem=head_send_sem.at[step],
-            recv_sem=head_recv_sem.at[step],
+        pltpu.make_async_remote_copy(
+            src_ref=square_send.at[pl.ds(0, pairs + 1)],
+            dst_ref=square_recv.at[step - 1, pl.ds(0, pairs + 1)],
+            send_sem=head_send_sem,
+            recv_sem=head_recv_sem,
             device_id=(me, lax.rem(me_head + step, n_head)),
             device_id_type=MESH,
-        )
-        copy.start()
-        head_copies.append((step, copy))
+        ).start()
+    if n_head > 1:
+        used = square_recv.at[:, pl.ds(0, pairs + 1)]
+        pltpu.make_async_copy(used, used, head_recv_sem).wait()
     summed = square_send[...]
-    for step, copy in reversed(head_copies):
-        copy.wait_recv()
-        summed = summed + square_recv[step]
-    inverse = 1.0 / jnp.sqrt(summed * (1.0 / (HEADS * HD)) + 1e-6)
-    root_buf[...] = jnp.concatenate([inverse, jnp.zeros((HD - kept, rows), F32)], axis=0).T
-
-    gain = gain_buf[...].astype(F32).reshape(1, heads * HD)
-    outs = []
+    for step in range(1, n_head):
+        summed = summed + square_recv[step - 1]
+    used_rows = lax.broadcasted_iota(jnp.int32, summed.shape, 0) <= pairs
+    mean = jnp.where(used_rows, summed, 0.0) * (1.0 / (HEADS * HD))
+    inverse = 1.0 / jnp.sqrt(mean + 1e-6)
+    gain = gain_buf[...].astype(F32).reshape(1, width)
+    roots = jnp.concatenate([inverse, jnp.zeros((HD - kept, rows), F32)], axis=0).T
     for pair in range(pairs, -1, -1):
-        scale = root_buf[:, pair : pair + 1]
-        staged[pair] = (total[pair] * scale * gain).astype(BF16)
         target = slab_out if pair == pairs else user_out.at[pair]
-        out = pltpu.make_async_copy(staged.at[pair], target, out_sem.at[pair])
-        out.start()
-        outs.append(out)
-    for copy in copies:
-        copy.wait_send()
-    for _, copy in head_copies:
-        copy.wait_send()
-    for out in outs:
-        out.wait()
+        target[...] = (total[pair] * roots[:, pair : pair + 1] * gain).astype(BF16)
+    for link in LINKS:
+        if sent_rows[link]:
+            rows_copy(sent_rows[link], send_sem.at[LINKS.index(link)]).wait()
+    if n_head > 1:
+        pltpu.make_async_copy(used, used, head_send_sem).wait()
 
 
 def local(
@@ -451,7 +455,10 @@
     depth = n_seq.bit_length() - 1
     paired = (pairs, 2 * suffix, width)
     whole = pl.BlockSpec(memory_space=pl.ANY)
-    slot_count = n_seq * len(UNITS)
+    nx = 1 << (depth // 2)
+    pieces = plan_gather(nx, n_seq // nx, 0)[2]
+    relayed = [key for key in pieces if key[1:] != (0, 0) and forwards(nx, n_seq // nx, *key)]
+    recv_count = len(relayed) + len(UNITS)
     buffers = (pairs + 1, tokens, width)
     kept = -(-(pairs + 1) // 8) * 8
     slab_out, user_out = pl.pallas_call(
@@ -461,7 +468,7 @@
             jax.ShapeDtypeStruct(paired, BF16),
         ),
         in_specs=[whole] * 10,
-        out_specs=(whole, whole),
+        out_specs=(pl.BlockSpec(memory_space=pltpu.VMEM),) * 2,
         scratch_shapes=[
             pltpu.SMEM(prefix_lengths.shape, jnp.int32),
             pltpu.VMEM(buffers, BF16),
@@ -470,20 +477,17 @@
             pltpu.VMEM(slab_levels.shape, BF16),
             pltpu.VMEM(user_levels.shape, BF16),
             pltpu.VMEM(norm_gain.shape, BF16),
-            pltpu.VMEM((n_seq, width, HD), BF16),
+            pltpu.VMEM((n_seq * width, HD), BF16),
             pltpu.VMEM((heads, n_seq - 1, HD, HD), BF16),
             pltpu.VMEM((pairs + 1, heads, tokens, depth * HD), BF16),
             pltpu.VMEM(buffers, F32),
-            pltpu.VMEM(buffers, BF16),
             pltpu.VMEM((kept, tokens), F32),
-            pltpu.VMEM((n_head, kept, tokens), F32),
-            pltpu.VMEM((tokens, HD), F32),
+            pltpu.VMEM((max(n_head - 1, 1), kept, tokens), F32),
             pltpu.SemaphoreType.DMA((10,)),
-            pltpu.SemaphoreType.DMA((pairs + 1,)),
-            pltpu.SemaphoreType.DMA((slot_count,)),
-            pltpu.SemaphoreType.DMA((slot_count,)),
-            pltpu.SemaphoreType.DMA((n_head,)),
-            pltpu.SemaphoreType.DMA((n_head,)),
+            pltpu.SemaphoreType.DMA((len(LINKS),)),
+            pltpu.SemaphoreType.DMA((recv_count,)),
+            pltpu.SemaphoreType.DMA,
+            pltpu.SemaphoreType.DMA,
         ],
         compiler_params=pltpu.CompilerParams(
             collective_id=0, has_side_effects=True, vmem_limit_bytes=50 * 1024 * 1024

time: 65.8 us -> 49.8 us (0.76)
  Pallas kernels: 63.4 us -> 47.4 us
    pallas_call x1, Pallas kernels: 63.4 us -> 47.4 us  [local(): pl.pallas_call(functools.partial(kernel, n_seq, n_head), out_shape=(jax.S...]
where the time goes in v2:
time: 49.8 us; the launch traced here: 49.7 us
  Pallas kernels  47.4 us (95%)
  local copies, waits for them, and re-layouts  1.63 us (3%)
  between operations  0.64 us (1%)
    pallas_call x1, Pallas kernels, local(): pl.pallas_call(functools.partial(kernel, n_seq, n_head), out_shape=(jax.S...  47.4 us
    unnamed x2, local copies, waits for them, and re-layouts  1.63 us

profile of v2, /device:TPU:1, one launch (start us, length us, event | category | flops | bytes accessed | tf_op | source)
XLA Modules:
  0.0 49.7 jit_solution(6582074929735336129)
XLA Ops:
  0.6 47.4 %shard_map.113 = (bf16[128,512]{1,0:T(8,128)(2,1)S(1)}, bf16[8,128,512]{2,1,0:T(8,128)(2,1)S(1)}) custom-call(s32[16]{0:T(128)} %prefix_hbm.1, bf16[128,512]{1,0:T(8,128)(2,1)} %slab_q.1, bf16[128,512]{1,0:T(8,128)(2,1)} %slab_k.1, bf16[128,512]{1,0:T(8,128)(2,1)} %slab_v.1, bf16[6,4,128]{2,1,0:T(4,128)(2,1)} %slab_w.1, bf16[512]{0:T(512)(128)(2,1)} %gain_hbm.1, ...), custom_call_target="tpu_custom_call" | custom-call | tf_op jit(solution)/shard_map/pallas_call | solution.py:464
  48.1 0.7 %copy.14 = bf16[128,512]{1,0:T(8,128)(2,1)} copy(bf16[128,512]{1,0:T(8,128)(2,1)S(1)} %get-tuple-element.8) | data formatting | bytes 262144
  48.7 1.0 %copy.15 = bf16[16,64,512]{2,1,0:T(8,128)(2,1)} copy(bf16[16,64,512]{2,1,0:T(8,128)(2,1)S(1)} %bitcast.4) | data formatting | bytes 2097152

commit v3 on v2

--- a/solution.py
+++ b/solution.py
@@ -27,7 +27,10 @@
 HOP_US = 2.6
 ISSUE_AHEAD_US = 0.5
 PRIORITY_WEIGHT = 0.3
-WORK_US = 0.4
+WORK_US = 0.3
+WORK_GAP = 0.8
+GREET_FROM_US = 10.0
+GREET_EVERY_US = 3.0
 
 
 def reach(ring, plus):
@@ -63,7 +66,7 @@
     return result
 
 
-def plan_gather(nx, ny, work_count):
+def plan_gather(nx, ny, work_count, rounds):
     def depth(key):
         return max([1 + depth((key[0], a, b)) for _, a, b in forwards(nx, ny, *key)], default=0)
 
@@ -97,16 +100,20 @@
 
     arrival = dict.fromkeys(own, 0.0)
     free = dict.fromkeys(LINKS, 0.0)
-    steps, now, work = [], 0.0, 0
+    steps, now, work, greetings = [], 0.0, 0, 0
     for _, _, link, key, target in sorted(sends):
-        while work < work_count and arrival[key] - now > 0.6 * WORK_US:
+        while work < work_count and arrival[key] - now > WORK_GAP * WORK_US:
             steps.append(("work", work))
             work, now = work + 1, now + WORK_US
         now = max(now, arrival[key])
+        if greetings < rounds and now > GREET_FROM_US + GREET_EVERY_US * greetings:
+            steps.append(("greet", greetings))
+            greetings += 1
         free[link] = max(now, free[link]) + send_us(key[0])
         arrival[target] = free[link] + HOP_US
         steps.append(("send", (link, key, target)))
     steps += [("work", index) for index in range(work, work_count)]
+    steps += [("greet", index) for index in range(greetings, rounds)]
     complete = [
         max(time for key, time in arrival.items() if key[0] in units) for units in HEAD_UNITS
     ]
@@ -147,6 +154,7 @@
     recv_sem,
     head_send_sem,
     head_recv_sem,
+    greet_sem,
 ):
     pairs = user_q.shape[0]
     width = q_buf.shape[2]
@@ -164,11 +172,9 @@
         return lax.rem(x + (dx + nx), nx) * ny + lax.rem(y + (dy + ny), ny)
 
     loads = [
-        pltpu.make_async_copy(source, target, in_sem.at[index])
+        pltpu.make_async_copy(source, target, in_sem.at[heads + index])
         for index, (source, target) in enumerate(
             (
-                (slab_k, k_buf.at[pairs]),
-                (slab_v, v_buf.at[pairs]),
                 (slab_q, q_buf.at[pairs]),
                 (slab_w, slab_w_buf),
                 (prefix_hbm, prefix_ref),
@@ -180,8 +186,12 @@
             )
         )
     ]
-    for load in loads[:2]:
-        load.start()
+    for head in range(heads):
+        lanes = slice(head * HD, (head + 1) * HD)
+        for source, target in ((slab_k, k_buf), (slab_v, v_buf)):
+            pltpu.make_async_copy(
+                source.at[:, lanes], target.at[pairs, :, lanes], in_sem.at[head]
+            ).start()
 
     neighbours = {
         "x+": block_at(1, 0),
@@ -189,35 +199,32 @@
         "y+": block_at(0, 1),
         "y-": block_at(0, -1),
     }
+    core, chip, chips = lax.rem(me_head, 2), me_head // 2, n_head // 2
+    beside = [
+        lax.rem(chip + step, chips) * 2 + core for step in sorted({1, chips - 1} - {0, chips})
+    ]
+    greeted = [(neighbours[link], me_head) for link in LINKS]
+    greeted += [(me, head) for head in beside]
+    if n_head > 1:
+        greeted.append((me, me_head + 1 - 2 * core))
     barrier = pltpu.get_barrier_semaphore()
-    for step in range(1, n_head):
-        pl.semaphore_signal(
-            barrier,
-            inc=1,
-            device_id=(me, lax.rem(me_head + step, n_head)),
-            device_id_type=MESH,
-        )
-    for link in neighbours:
-        pl.semaphore_signal(
-            barrier, inc=1, device_id=(neighbours[link], me_head), device_id_type=MESH
-        )
-
-    loads[0].wait()
-    loads[1].wait()
-    for head in range(heads):
-        lanes = slice(head * HD, (head + 1) * HD)
-        state = lax.dot_general(
-            k_buf[pairs, :, lanes],
-            v_buf[pairs, :, lanes],
-            (((0,), (0,)), ((), ())),
-            preferred_element_type=F32,
-        )
-        blocks[pl.ds(pl.multiple_of(me * width + head * HD, HD), HD), :] = state.astype(BF16)
-    for load in loads[2:]:
+    for device in greeted:
+        pl.semaphore_signal(barrier, inc=1, device_id=device, device_id_type=MESH)
+
+    def greet(index):
+        for head in beside:
+            pl.semaphore_signal(
+                greet_sem.at[index], inc=1, device_id=(me, head), device_id_type=MESH
+            )
+
+    for load in loads:
         load.start()
-    pl.semaphore_wait(barrier, n_head - 1 + len(neighbours))
-
-    steps, head_order, pieces = plan_gather(nx, ny, 3 * (pairs + 1))
+    pl.semaphore_wait(barrier, len(greeted))
+    rounds = chips // 2
+    if rounds:
+        greet(0)
+
+    steps, head_order, pieces = plan_gather(nx, ny, (heads + 2) * (pairs + 1), rounds)
     relayed = [key for key in pieces if key[1:] != (0, 0) and forwards(nx, ny, *key)]
     kept_pieces = [key for key in pieces if not forwards(nx, ny, *key)]
     slots = {key: index for index, key in enumerate(relayed)}
@@ -270,19 +277,16 @@
                     :, head * HD : (head + 1) * HD
                 ]
 
-    def scale_piece(pair):
+    def scale_piece(pair, half):
+        first = half * suffix
         if pair == pairs:
-            scale_rows(pair, 0, rows, lambda level: slab_w_buf[level], me)
+            tokens = slice(first, first + suffix)
+            scale_rows(pair, first, suffix, lambda level: slab_w_buf[level, :, tokens], me)
         else:
-            for half in range(2):
-                user = 2 * pair + half
-                scale_rows(
-                    pair,
-                    half * suffix,
-                    suffix,
-                    lambda level: user_w_buf[user, level],
-                    prefix_ref[user],
-                )
+            user = 2 * pair + half
+            scale_rows(
+                pair, first, suffix, lambda level: user_w_buf[user, level], prefix_ref[user]
+            )
 
     def local_piece(pair, group):
         group_lanes = slice(group[0] * HD, (group[-1] + 1) * HD)
@@ -356,7 +360,7 @@
 
     def read_pair(pair, head):
         lanes = slice(head * HD, (head + 1) * HD)
-        if pair is None:
+        if pair == pairs:
             total[pairs, :, lanes] += read_rows(pairs, head, 0, rows, me)
         else:
             for half in range(2):
@@ -367,23 +371,41 @@
 
     work_items = []
     for pair in range(pairs, -1, -1):
-        work_items.append(functools.partial(scale_piece, pair))
-        for group in (range(heads // 2), range(heads // 2, heads)):
-            work_items.append(functools.partial(local_piece, pair, group))
-
+        for half in range(2):
+            work_items.append(functools.partial(scale_piece, pair, half))
+        for head in range(heads):
+            work_items.append(functools.partial(local_piece, pair, (head,)))
+
+    for head in range(heads):
+        rows_copy(2 * rows, in_sem.at[head]).wait()
+    for head in range(heads):
+        lanes = slice(head * HD, (head + 1) * HD)
+        state = lax.dot_general(
+            k_buf[pairs, :, lanes],
+            v_buf[pairs, :, lanes],
+            (((0,), (0,)), ((), ())),
+            preferred_element_type=F32,
+        )
+        blocks[pl.ds(pl.multiple_of(me * width + head * HD, HD), HD), :] = state.astype(BF16)
     loaded = False
     sent_rows = dict.fromkeys(LINKS, 0)
     for kind, item in steps:
         if kind == "work":
-            for load in () if loaded else loads[2:]:
+            for load in () if loaded else loads:
                 load.wait()
             loaded = True
             work_items[item]()
+        elif kind == "greet":
+            pl.semaphore_wait(greet_sem.at[item], len(beside))
+            if item + 1 < rounds:
+                greet(item + 1)
         else:
             link, key, target = item
             await_piece(key)
             piece_copy(link, key, target).start()
             sent_rows[link] += UNITS[key[0]][1]
+    lane_ids = lax.broadcasted_iota(jnp.int32, (rows, HD), 1)
+    squares = jnp.zeros((rows, HD), F32)
     for head in head_order:
         for unit in HEAD_UNITS[head]:
             for key in relayed:
@@ -392,17 +414,13 @@
             kept_rows = UNITS[unit][1] * sum(key[0] == unit for key in kept_pieces)
             rows_copy(kept_rows, recv_sem.at[len(slots) + unit]).wait()
         build_nodes(head)
-        read_pair(None, head)
-        for pair in range(pairs):
+        for pair in range(pairs, -1, -1):
             read_pair(pair, head)
-
-    lane_ids = lax.broadcasted_iota(jnp.int32, (rows, HD), 1)
-    squares = jnp.zeros((rows, HD), F32)
-    for pair in range(pairs + 1):
-        values = total[pair]
-        values = values * values
-        column = jnp.sum(values, axis=1, keepdims=True)
-        squares = jnp.where(lane_ids == pair, column, squares)
+            if head == head_order[-1]:
+                values = total[pair]
+                column = jnp.sum(values * values, axis=1, keepdims=True)
+                squares = jnp.where(lane_ids == pair, column, squares)
+
     kept = square_send.shape[0]
     square_send[...] = squares.T[:kept]
     for step in sorted(range(1, n_head), key=lambda s: -min(s, n_head - s)):
@@ -456,7 +474,7 @@
     paired = (pairs, 2 * suffix, width)
     whole = pl.BlockSpec(memory_space=pl.ANY)
     nx = 1 << (depth // 2)
-    pieces = plan_gather(nx, n_seq // nx, 0)[2]
+    pieces = plan_gather(nx, n_seq // nx, 0, 0)[2]
     relayed = [key for key in pieces if key[1:] != (0, 0) and forwards(nx, n_seq // nx, *key)]
     recv_count = len(relayed) + len(UNITS)
     buffers = (pairs + 1, tokens, width)
@@ -483,11 +501,12 @@
             pltpu.VMEM(buffers, F32),
             pltpu.VMEM((kept, tokens), F32),
             pltpu.VMEM((max(n_head - 1, 1), kept, tokens), F32),
-            pltpu.SemaphoreType.DMA((10,)),
+            pltpu.SemaphoreType.DMA((heads + 8,)),
             pltpu.SemaphoreType.DMA((len(LINKS),)),
             pltpu.SemaphoreType.DMA((recv_count,)),
             pltpu.SemaphoreType.DMA,
             pltpu.SemaphoreType.DMA,
+            pltpu.SemaphoreType.REGULAR((max(n_head // 4, 1),)),
         ],
         compiler_params=pltpu.CompilerParams(
             collective_id=0, has_side_effects=True, vmem_limit_bytes=50 * 1024 * 1024

time: 49.8 us -> 48.2 us (0.968)
  Pallas kernels: 47.4 us -> 45.8 us
    pallas_call x1, Pallas kernels: 47.4 us -> 45.8 us  [local(): pl.pallas_call(functools.partial(kernel, n_seq, n_head), out_shape=(jax.S...]
where the time goes in v3:
time: 48.2 us; the launch traced here: 48.1 us
  Pallas kernels  45.8 us (95%)
  local copies, waits for them, and re-layouts  1.63 us (3%)
  between operations  0.64 us (1%)
    pallas_call x1, Pallas kernels, local(): pl.pallas_call(functools.partial(kernel, n_seq, n_head), out_shape=(jax.S...  45.8 us
    unnamed x2, local copies, waits for them, and re-layouts  1.63 us

profile of v3, /device:TPU:1, one launch (start us, length us, event | category | flops | bytes accessed | tf_op | source)
XLA Modules:
  0.0 48.1 jit_solution(2428512538506315433)
XLA Ops:
  0.6 45.8 %shard_map.113 = (bf16[128,512]{1,0:T(8,128)(2,1)S(1)}, bf16[8,128,512]{2,1,0:T(8,128)(2,1)S(1)}) custom-call(s32[16]{0:T(128)} %prefix_hbm.1, bf16[128,512]{1,0:T(8,128)(2,1)} %slab_q.1, bf16[128,512]{1,0:T(8,128)(2,1)} %slab_k.1, bf16[128,512]{1,0:T(8,128)(2,1)} %slab_v.1, bf16[6,4,128]{2,1,0:T(4,128)(2,1)} %slab_w.1, bf16[512]{0:T(512)(128)(2,1)} %gain_hbm.1, ...), custom_call_target="tpu_custom_call" | custom-call | tf_op jit(solution)/shard_map/pallas_call | solution.py:482
  46.4 0.7 %copy.14 = bf16[128,512]{1,0:T(8,128)(2,1)} copy(bf16[128,512]{1,0:T(8,128)(2,1)S(1)} %get-tuple-element.8) | data formatting | bytes 262144
  47.1 1.0 %copy.15 = bf16[16,64,512]{2,1,0:T(8,128)(2,1)} copy(bf16[16,64,512]{2,1,0:T(8,128)(2,1)S(1)} %bitcast.4) | data formatting | bytes 2097152
